TPU v7x, 32 devices: a whole 2x2x4 slice. The times are simulated.
32 devices in a mesh: gx: 4 (over y, core), gy: 8 (over z, x).
Axes of the slice: x: 2, y: 2, z: 4, core: 2. Of those that a mesh axis runs over, the one named last changes fastest.
Arguments:
- source: float32 [256, 128, 128], P('gx', 'gy'), may hold values from -6 to 6
- diagonal: float32 [256, 128, 128], P('gx', 'gy'), may hold values from 6.05 to 7
- face_x: float32 [256, 128, 128], P('gx', 'gy'), may hold values from 0.1 to 1
- face_y: float32 [256, 128, 128], P('gx', 'gy'), may hold values from 0.1 to 1
- face_z: float32 [256, 128, 128], P('gx', 'gy'), may hold values from 0.1 to 1
- iterates: float32 [8, 256, 128, 128], P(None, 'gx', 'gy'), may hold values from -0.3 to 0.3
- labels: int32 [256, 128], P('gx', 'gy'), may hold values from 0 to 7
Outputs:
- new_iterates: float32 [8, 256, 128, 128], P(None, 'gx', 'gy')
- new_residual: float32 [256, 128, 128], P('gx', 'gy')
All inputs are finite; a program needn't handle non-finite values.
Results may differ from a plain program's by a relative error of at most 0.0003.
Values sent between devices are 32-bit elements; how exact they have to be, the bound alone decides.
No kernel may reach another device: no remote copies, remote signals or barrier semaphores. Data moves between devices by JAX's collectives and lax.ppermute only.
A program may use at most 128 MiB of HBM per device.

v0:
```python
import jax
import jax.numpy as jnp
from jax import lax
from jax.sharding import PartitionSpec as P

ENLARGE = 8
basis_shift = 6.5


def padded_2(block, sides, width):
    for axis, dim in sides:
        count = lax.axis_size(axis)
        forward = [(i, i + 1) for i in range(count - 1)]
        backward = [(target, source) for source, target in forward]
        low = lax.ppermute(
            lax.slice_in_dim(block, block.shape[dim] - width, None, axis=dim), axis, forward
        )
        high = lax.ppermute(lax.slice_in_dim(block, 0, width, axis=dim), axis, backward)
        block = jnp.concatenate([low, block, high], axis=dim)
    return block


def stencil(values, face_x, face_y, face_z, diagonal):
    centre = values[..., 1:-1, 1:-1, :]
    result = diagonal * centre
    result = (
        result
        - face_x[1:-1, 1:-1, :] * values[..., 2:, 1:-1, :]
        - face_x[:-2, 1:-1, :] * values[..., :-2, 1:-1, :]
    )
    result = (
        result
        - face_y[1:-1, 1:-1, :] * values[..., 1:-1, 2:, :]
        - face_y[1:-1, :-2, :] * values[..., 1:-1, :-2, :]
    )
    widths = [(0, 0)] * (centre.ndim - 1) + [(1, 1)]
    padded = jnp.pad(centre, widths)
    lower_face = jnp.pad(face_z[..., :-1], ((0, 0), (0, 0), (1, 0)))
    return result - face_z * padded[..., 2:] - lower_face * padded[..., :-2]


def finish(gram, project):
    highest = lax.Precision.HIGHEST
    lower = jnp.linalg.cholesky(gram)
    ident = jnp.eye(gram.shape[0], dtype=gram.dtype)
    inverse = lax.linalg.triangular_solve(lower, ident, left_side=True, lower=True)
    reduced = jnp.dot(jnp.dot(inverse, project, precision=highest), inverse.T, precision=highest)
    reduced = 0.5 * (reduced + reduced.T)
    target = jnp.dot(inverse, gram[:, :ENLARGE], precision=highest)
    factor = jnp.linalg.cholesky(reduced)
    middle = lax.linalg.triangular_solve(factor, target, left_side=True, lower=True)
    solved = lax.linalg.triangular_solve(
        factor, middle, left_side=True, lower=True, transpose_a=True
    )
    return jnp.dot(inverse.T, solved, precision=highest)


def shards(source, diagonal, face_x, face_y, face_z, iterates, labels):
    highest = lax.Precision.HIGHEST
    summed = jnp.sum(iterates, axis=0)
    columns = jnp.arange(ENLARGE, dtype=jnp.int32)
    near = (
        padded_2(summed, (("gx", 0), ("gy", 1)), 1),
        padded_2(face_x, (("gx", 0), ("gy", 1)), 1),
        padded_2(face_y, (("gx", 0), ("gy", 1)), 1),
    )
    near_sum, near_fx, near_fy = near
    residual = source - stencil(near_sum, near_fx, near_fy, face_z, diagonal)
    onehot = (labels[None] == columns[:, None, None]).astype(jnp.float32)
    blocks = residual[None] * onehot[..., None]
    blocks_wide = padded_2(blocks, (("gx", 1), ("gy", 2)), 1)
    applied = stencil(blocks_wide, near_fx, near_fy, face_z, diagonal)
    powered = applied - basis_shift * blocks
    powered_wide = padded_2(powered, (("gx", 1), ("gy", 2)), 1)
    second = stencil(powered_wide, near_fx, near_fy, face_z, diagonal)
    basis = jnp.concatenate([blocks, powered], axis=0)
    image = jnp.concatenate([applied, second], axis=0)
    gram_local = jnp.einsum("aijk,bijk->ab", basis, basis, precision=highest)
    project_local = jnp.einsum("aijk,bijk->ab", basis, image, precision=highest)
    gram = lax.psum(gram_local, ("gx", "gy"))
    project = lax.psum(project_local, ("gx", "gy"))
    coeffs = finish(gram, project)
    new_iterates = iterates + jnp.einsum("ab,aijk->bijk", coeffs, basis, precision=highest)
    carried = jnp.sum(coeffs, axis=1)
    new_residual = residual - jnp.einsum("a,aijk->ijk", carried, image, precision=highest)
    return (new_iterates, new_residual)


def solution(mesh):
    placed = (
        P("gx", "gy", None),
        P("gx", "gy", None),
        P("gx", "gy", None),
        P("gx", "gy", None),
        P("gx", "gy", None),
        P(None, "gx", "gy", None),
        P("gx", "gy"),
    )
    return jax.shard_map(
        shards,
        mesh=mesh,
        in_specs=placed,
        out_specs=(P(None, "gx", "gy", None), P("gx", "gy", None)),
        check_vma=False,
    )
```

profile of v0, /device:TPU:0, one launch (start us, length us, event | category | flops | bytes accessed | tf_op | source)
XLA Modules:
  0.0 177.3 jit_solution(15040397435094770270)
XLA Ops:
  0.7 2.7 %reduce_sum.18 = f32[64,16,128]{2,1,0:T(8,128)S(1)} reduce(f32[8,64,16,128]{3,2,1,0:T(8,128)} %param.13, f32[]{:T(128)} %constant.43.clone.1), dimensions={0}, to_apply=%region_0.0 | reduce | flops 917504 | bytes 4718596 | tf_op jit(solution)/shard_map/reduce_sum | solution.py:60
  3.4 1.3 collective-permute-start
  4.7 3.0 %collective-permute-start.2 = (f32[1,16,128]{2,1,0:T(8,128)S(1)}, f32[1,16,128]{2,1,0:T(8,128)S(1)}, u32[]{:S(2)}, u32[]{:S(2)}) collective-permute-start(f32[1,16,128]{2,1,0:T(8,128)S(1)} %get-tuple-element.23), channel_id=1, source_target_pairs={{0,8},{8,16},{16,24},{1,9},{9,17},{17,25},{2,10},{10,18},{18,26},{... | collective-permute-start | bytes 24584 | tf_op jit(solution)/shard_map/ppermute | solution.py:15
  7.7 4.5 %collective-permute-start.4 = (f32[1,16,128]{2,1,0:T(8,128)S(1)}, f32[1,16,128]{2,1,0:T(8,128)S(1)}, u32[]{:S(2)}, u32[]{:S(2)}) collective-permute-start(f32[1,16,128]{2,1,0:T(8,128)S(1)} %get-tuple-element.22), channel_id=1, source_target_pairs={{0,8},{8,16},{16,24},{1,9},{9,17},{17,25},{2,10},{10,18},{18,26},{... | collective-permute-start | bytes 24584 | tf_op jit(solution)/shard_map/ppermute | solution.py:15
  12.2 1.3 collective-permute-start.5
  13.6 3.0 %collective-permute-start.1 = (f32[1,16,128]{2,1,0:T(8,128)S(1)}, f32[1,16,128]{2,1,0:T(8,128)S(1)}, u32[]{:S(2)}, u32[]{:S(2)}) collective-permute-start(f32[1,16,128]{2,1,0:T(8,128)S(1)} %slice.156), channel_id=1, source_target_pairs={{0,8},{8,16},{16,24},{1,9},{9,17},{17,25},{2,10},{10,18},{18,26},{... | collective-permute-start | bytes 24584 | tf_op jit(solution)/shard_map/ppermute | solution.py:15
  16.8 1.3 collective-permute-start.3
  18.1 4.5 %collective-permute-start.7 = (f32[66,1,128]{2,1,0:T(1,128)S(1)}, f32[66,1,128]{2,1,0:T(1,128)S(1)}, u32[]{:S(2)}, u32[]{:S(2)}) collective-permute-start(f32[66,1,128]{2,1,0:T(1,128)S(1)} %get-tuple-element.20), channel_id=1, source_target_pairs={{0,1},{1,2},{2,3},{3,4},{4,5},{5,6},{6,7},{8,9},{9,10},{10,11},{11... | collective-permute-start | bytes 101384 | tf_op jit(solution)/shard_map/ppermute | solution.py:15
  22.7 4.3 %collective-permute-start.6 = (f32[66,1,128]{2,1,0:T(1,128)S(1)}, f32[66,1,128]{2,1,0:T(1,128)S(1)}, u32[]{:S(2)}, u32[]{:S(2)}) collective-permute-start(f32[66,1,128]{2,1,0:T(1,128)S(1)} %slice.194), channel_id=1, source_target_pairs={{0,1},{1,2},{2,3},{3,4},{4,5},{5,6},{6,7},{8,9},{9,10},{10,11},{11... | collective-permute-start | bytes 101384 | tf_op jit(solution)/shard_map/ppermute | solution.py:15
  27.3 1.3 collective-permute-done.6
  28.6 1.6 fusion.33
  31.5 1.3 collective-permute-start.8
  32.8 3.0 %collective-permute-start.9 = (f32[8,1,16,128]{3,0,2,1:T(8,128)S(1)}, f32[8,1,16,128]{3,0,2,1:T(8,128)S(1)}, u32[]{:S(2)}, u32[]{:S(2)}) collective-permute-start(f32[8,1,16,128]{3,0,2,1:T(8,128)S(1)} %get-tuple-element.17), channel_id=1, source_target_pairs={{0,8},{8,16},{16,24},{1,9},{9,17},{17,25},{2,10},{10,18},{18,26},{... | collective-permute-start | bytes 196616 | tf_op jit(solution)/shard_map/ppermute | solution.py:15
  36.8 1.3 collective-permute-start.10
  38.1 5.0 %collective-permute-start.11 = (f32[8,66,1,128]{3,0,2,1:T(8,128)S(1)}, f32[8,66,1,128]{3,0,2,1:T(8,128)S(1)}, u32[]{:S(2)}, u32[]{:S(2)}) collective-permute-start(f32[8,66,1,128]{3,0,2,1:T(8,128)S(1)} %get-tuple-element.14), channel_id=1, source_target_pairs={{0,1},{1,2},{2,3},{3,4},{4,5},{5,6},{6,7},{8,9},{9,10},{10,11},{11... | collective-permute-start | bytes 811016 | tf_op jit(solution)/shard_map/ppermute | solution.py:15
  43.4 4.0 %collective-permute-done.10 = f32[8,66,1,128]{3,0,2,1:T(8,128)S(1)} collective-permute-done((f32[8,66,1,128]{3,0,2,1:T(8,128)S(1)}, f32[8,66,1,128]{3,0,2,1:T(8,128)S(1)}, u32[]{:S(2)}, u32[]{:S(2)}) %collective-permute-start.10) | collective-permute-done | bytes 270368 | tf_op jit(solution)/shard_map/ppermute | solution.py:18
  47.4 7.2 %collective-permute-done.11 = f32[8,66,1,128]{3,0,2,1:T(8,128)S(1)} collective-permute-done((f32[8,66,1,128]{3,0,2,1:T(8,128)S(1)}, f32[8,66,1,128]{3,0,2,1:T(8,128)S(1)}, u32[]{:S(2)}, u32[]{:S(2)}) %collective-permute-start.11) | collective-permute-done | bytes 270368 | tf_op jit(solution)/shard_map/ppermute | solution.py:15
  54.6 7.5 %multiply_subtract_fusion = (f32[8,64,16,128]{3,0,2,1:T(8,128)S(1)}, f32[8,64,16,128]{3,0,2,1:T(8,128)S(1)}) fusion(f32[8,64,16]{0,2,1:T(8,128)S(1)} %fusion.43, f32[64,16,128]{2,1,0:T(8,128)S(1)} %get-tuple-element.9, f32[64,16,128]{2,1,0:T(8,128)S(1)} %pad.18, f32[8,64,16,128]{3,0,2,1:T(8,128)S(1)} %broadcast_multiply_fusion, ...), kind=kLoop, calls=%fused_computation.51 | loop fusion | flops 25165824 | bytes 17481728 | tf_op jit(solution)/shard_map/sub | solution.py:73
  62.1 1.3 collective-permute-start.12
  63.4 3.0 %collective-permute-start.13 = (f32[8,1,16,128]{3,0,2,1:T(8,128)S(1)}, f32[8,1,16,128]{3,0,2,1:T(8,128)S(1)}, u32[]{:S(2)}, u32[]{:S(2)}) collective-permute-start(f32[8,1,16,128]{3,0,2,1:T(8,128)S(1)} %get-tuple-element.15), channel_id=1, source_target_pairs={{0,8},{8,16},{16,24},{1,9},{9,17},{17,25},{2,10},{10,18},{18,26},{... | collective-permute-start | bytes 196616 | tf_op jit(solution)/shard_map/ppermute | solution.py:15
  67.4 1.3 collective-permute-start.14
  68.7 5.0 %collective-permute-start.15 = (f32[8,66,1,128]{3,0,2,1:T(8,128)S(1)}, f32[8,66,1,128]{3,0,2,1:T(8,128)S(1)}, u32[]{:S(2)}, u32[]{:S(2)}) collective-permute-start(f32[8,66,1,128]{3,0,2,1:T(8,128)S(1)} %get-tuple-element.12), channel_id=1, source_target_pairs={{0,1},{1,2},{2,3},{3,4},{4,5},{5,6},{6,7},{8,9},{9,10},{10,11},{11... | collective-permute-start | bytes 811016 | tf_op jit(solution)/shard_map/ppermute | solution.py:15
  73.7 11.2 %fusion.28 = f32[16,16]{0,1:T(8,128)S(1)} fusion(f32[8,64,16,128]{3,0,2,1:T(8,128)S(1)} %get-tuple-element.7, f32[8,64,16,128]{3,0,2,1:T(8,128)S(1)} %broadcast_multiply_fusion), kind=kOutput, calls=%fused_computation.55 | convolution fusion | flops 404750336 | bytes 8389632 | tf_op jit(solution)/shard_map/aijk,bijk->ab/dot_general | solution.py:78
  85.3 6.8 %fusion.10 = f32[8,64,16,128]{3,0,2,1:T(8,128)S(1)} fusion(f32[8,64,16,128]{3,0,2,1:T(8,128)S(1)} %get-tuple-element.7, f32[8,66,1,128]{3,0,2,1:T(8,128)S(1)} %collective-permute-done.15, f32[8,1,16,128]{3,0,2,1:T(8,128)S(1)} %collective-permute-done.12, f32[8,1,16,128]{3,0,2,1:T(8,128)S(1)} %collective-permute-done.13, ...), kind=kLoop, calls=%fused_computation.16 | loop fusion | flops 22020096 | bytes 12730368 | tf_op jit(solution)/shard_map/sub | solution.py:39
  92.1 1.9 %copy-done.5 = f32[8,64,16,128]{3,0,2,1:T(8,128)} copy-done((f32[8,64,16,128]{3,0,2,1:T(8,128)}, f32[8,64,16,128]{3,0,2,1:T(8,128)S(1)}, u32[]{:S(2)}) %copy-start.5) | copy-done | bytes 4194328
  94.1 10.4 %fusion.29 = f32[16,16]{1,0:T(8,128)S(1)} fusion(f32[8,64,16,128]{3,0,2,1:T(8,128)S(1)} %fusion.10, f32[8,64,16,128]{3,0,2,1:T(8,128)S(1)} %get-tuple-element.8, f32[8,64,16,128]{3,0,2,1:T(8,128)S(1)} %get-tuple-element.7, f32[8,64,16,128]{3,0,2,1:T(8,128)S(1)} %broadcast_multiply_fusion), kind=kOutput, calls=%fused_computation.56 | convolution fusion | flops 406847488 | bytes 16778240 | tf_op jit(solution)/shard_map/aijk,bijk->ab/dot_general | solution.py:79
  104.5 44.6 %all-reduce.4 = (f32[16,16]{0,1:T(8,128)S(1)}, f32[16,16]{1,0:T(8,128)S(1)}) all-reduce(f32[16,16]{0,1:T(8,128)S(1)} %fusion.28, f32[16,16]{1,0:T(8,128)S(1)} %fusion.29), channel_id=1, replica_groups=mesh['gx'=4,'gy'=8] {'gx','gy'}, use_global_device_ids=true, to_apply=%region_1.2 | all-reduce | flops 512 | bytes 4096 | tf_op jit(solution)/shard_map/psum | solution.py:80
  149.1 1.5 cholesky.44
  153.9 1.5 cholesky.55
  158.5 6.6 %fusion = f32[1,64,16,128]{3,0,2,1:T(1,128)S(1)} fusion(f32[8,64,16,128]{3,0,2,1:T(8,128)} %copy-done.5, f32[8,64,16,128]{3,0,2,1:T(8,128)} %copy-done.4, f32[16]{0:T(128)S(1)} %get-tuple-element.25), kind=kOutput, calls=%fused_computation.6 | convolution fusion | flops 27262976 | bytes 8912960 | tf_op jit(solution)/shard_map/a,aijk->ijk/dot_general | solution.py:85
  166.0 8.6 %copy_add_fusion = f32[8,64,16,128]{3,0,2,1:T(8,128)S(1)} fusion(f32[8,64,16,128]{3,2,1,0:T(8,128)} %param.13, f32[8,64,16,128]{3,0,2,1:T(8,128)S(1)} %copy-done.3, f32[8,64,16,128]{3,0,2,1:T(8,128)S(1)} %copy-done.1, f32[16,8]{0,1:T(8,128)S(1)} %get-tuple-element.26), kind=kOutput, calls=%fused_computation.50 | convolution fusion | flops 204472320 | bytes 16777728 | tf_op jit(solution)/shard_map/ab,aijk->bijk/dot_general | solution.py:83
  174.6 2.8 %copy.15 = f32[8,64,16,128]{3,2,1,0:T(8,128)} copy(f32[8,64,16,128]{3,0,2,1:T(8,128)S(1)} %copy_add_fusion) | data formatting | bytes 8388608
  (73 shorter events, 11.6 us)
Async XLA Ops:
  0.6 7.1 %copy-start.7 = (f32[64,16,128]{2,1,0:T(8,128)S(1)}, f32[64,16,128]{2,1,0:T(8,128)}, u32[]{:S(2)}) copy-start(f32[64,16,128]{2,1,0:T(8,128)} %param.11) | copy-start | bytes 1572868
  0.6 12.9 %copy-start.8 = (f32[64,16,128]{2,1,0:T(8,128)S(1)}, f32[64,16,128]{2,1,0:T(8,128)}, u32[]{:S(2)}) copy-start(f32[64,16,128]{2,1,0:T(8,128)} %param.10) | copy-start | bytes 1572868
  0.7 15.9 %copy-start.10 = (s32[64,16]{0,1:T(8,128)S(1)}, s32[64,16]{0,1:T(8,128)}, u32[]{:S(2)}) copy-start(s32[64,16]{0,1:T(8,128)} %param.14) | copy-start | bytes 12292
  0.7 28.0 %copy-start.6 = (f32[64,16,128]{2,1,0:T(8,128)S(1)}, f32[64,16,128]{2,1,0:T(8,128)}, u32[]{:S(2)}) copy-start(f32[64,16,128]{2,1,0:T(8,128)} %param.12) | copy-start | bytes 1572868
  0.7 28.0 %copy-start.9 = (f32[64,16,128]{2,1,0:T(8,128)S(1)}, f32[64,16,128]{2,1,0:T(8,128)}, u32[]{:S(2)}) copy-start(f32[64,16,128]{2,1,0:T(8,128)} %param.9) | copy-start | bytes 1572868
  3.4 13.3 %collective-permute-start = (f32[1,16,128]{2,1,0:T(8,128)S(1)}, f32[1,16,128]{2,1,0:T(8,128)S(1)}, u32[]{:S(2)}, u32[]{:S(2)}) collective-permute-start(f32[1,16,128]{2,1,0:T(8,128)S(1)} %get-tuple-element.24), channel_id=1, source_target_pairs={{8,0},{16,8},{24,16},{9,1},{17,9},{25,17},{10,2},{18,10},{26,18},{... | collective-permute-start | bytes 24584 | tf_op jit(solution)/shard_map/ppermute | solution.py:18
  4.7 12.0 %collective-permute-start.2 = (f32[1,16,128]{2,1,0:T(8,128)S(1)}, f32[1,16,128]{2,1,0:T(8,128)S(1)}, u32[]{:S(2)}, u32[]{:S(2)}) collective-permute-start(f32[1,16,128]{2,1,0:T(8,128)S(1)} %get-tuple-element.23), channel_id=1, source_target_pairs={{0,8},{8,16},{16,24},{1,9},{9,17},{17,25},{2,10},{10,18},{18,26},{... | collective-permute-start | bytes 24584 | tf_op jit(solution)/shard_map/ppermute | solution.py:15
  7.7 14.9 %collective-permute-start.4 = (f32[1,16,128]{2,1,0:T(8,128)S(1)}, f32[1,16,128]{2,1,0:T(8,128)S(1)}, u32[]{:S(2)}, u32[]{:S(2)}) collective-permute-start(f32[1,16,128]{2,1,0:T(8,128)S(1)} %get-tuple-element.22), channel_id=1, source_target_pairs={{0,8},{8,16},{16,24},{1,9},{9,17},{17,25},{2,10},{10,18},{18,26},{... | collective-permute-start | bytes 24584 | tf_op jit(solution)/shard_map/ppermute | solution.py:15
  12.2 10.4 %collective-permute-start.5 = (f32[1,16,128]{2,1,0:T(8,128)S(1)}, f32[1,16,128]{2,1,0:T(8,128)S(1)}, u32[]{:S(2)}, u32[]{:S(2)}) collective-permute-start(f32[1,16,128]{2,1,0:T(8,128)S(1)} %get-tuple-element.21), channel_id=1, source_target_pairs={{8,0},{16,8},{24,16},{9,1},{17,9},{25,17},{10,2},{18,10},{26,18},{... | collective-permute-start | bytes 24584 | tf_op jit(solution)/shard_map/ppermute | solution.py:18
  13.6 13.7 %collective-permute-start.1 = (f32[1,16,128]{2,1,0:T(8,128)S(1)}, f32[1,16,128]{2,1,0:T(8,128)S(1)}, u32[]{:S(2)}, u32[]{:S(2)}) collective-permute-start(f32[1,16,128]{2,1,0:T(8,128)S(1)} %slice.156), channel_id=1, source_target_pairs={{0,8},{8,16},{16,24},{1,9},{9,17},{17,25},{2,10},{10,18},{18,26},{... | collective-permute-start | bytes 24584 | tf_op jit(solution)/shard_map/ppermute | solution.py:15
  16.8 10.5 %collective-permute-start.3 = (f32[66,1,128]{2,1,0:T(1,128)S(1)}, f32[66,1,128]{2,1,0:T(1,128)S(1)}, u32[]{:S(2)}, u32[]{:S(2)}) collective-permute-start(f32[66,1,128]{2,1,0:T(1,128)S(1)} %get-tuple-element.19), channel_id=1, source_target_pairs={{1,0},{2,1},{3,2},{4,3},{5,4},{6,5},{7,6},{9,8},{10,9},{11,10},{12... | collective-permute-start | bytes 101384 | tf_op jit(solution)/shard_map/ppermute | solution.py:18
  18.1 9.2 %collective-permute-start.7 = (f32[66,1,128]{2,1,0:T(1,128)S(1)}, f32[66,1,128]{2,1,0:T(1,128)S(1)}, u32[]{:S(2)}, u32[]{:S(2)}) collective-permute-start(f32[66,1,128]{2,1,0:T(1,128)S(1)} %get-tuple-element.20), channel_id=1, source_target_pairs={{0,1},{1,2},{2,3},{3,4},{4,5},{5,6},{6,7},{8,9},{9,10},{10,11},{11... | collective-permute-start | bytes 101384 | tf_op jit(solution)/shard_map/ppermute | solution.py:15
  22.7 5.9 %collective-permute-start.6 = (f32[66,1,128]{2,1,0:T(1,128)S(1)}, f32[66,1,128]{2,1,0:T(1,128)S(1)}, u32[]{:S(2)}, u32[]{:S(2)}) collective-permute-start(f32[66,1,128]{2,1,0:T(1,128)S(1)} %slice.194), channel_id=1, source_target_pairs={{0,1},{1,2},{2,3},{3,4},{4,5},{5,6},{6,7},{8,9},{9,10},{10,11},{11... | collective-permute-start | bytes 101384 | tf_op jit(solution)/shard_map/ppermute | solution.py:15
  31.5 60.6 %copy-start = (f32[8,64,16,128]{3,0,2,1:T(8,128)}, f32[8,64,16,128]{3,0,2,1:T(8,128)S(1)}, u32[]{:S(2)}) copy-start(f32[8,64,16,128]{3,0,2,1:T(8,128)S(1)} %broadcast_multiply_fusion) | copy-start | bytes 12582916
  31.5 4.3 %collective-permute-start.8 = (f32[8,1,16,128]{3,0,2,1:T(8,128)S(1)}, f32[8,1,16,128]{3,0,2,1:T(8,128)S(1)}, u32[]{:S(2)}, u32[]{:S(2)}) collective-permute-start(f32[8,1,16,128]{3,0,2,1:T(8,128)S(1)} %get-tuple-element.18), channel_id=1, source_target_pairs={{8,0},{16,8},{24,16},{9,1},{17,9},{25,17},{10,2},{18,10},{26,18},{... | collective-permute-start | bytes 196616 | tf_op jit(solution)/shard_map/ppermute | solution.py:18
  32.8 3.9 %collective-permute-start.9 = (f32[8,1,16,128]{3,0,2,1:T(8,128)S(1)}, f32[8,1,16,128]{3,0,2,1:T(8,128)S(1)}, u32[]{:S(2)}, u32[]{:S(2)}) collective-permute-start(f32[8,1,16,128]{3,0,2,1:T(8,128)S(1)} %get-tuple-element.17), channel_id=1, source_target_pairs={{0,8},{8,16},{16,24},{1,9},{9,17},{17,25},{2,10},{10,18},{18,26},{... | collective-permute-start | bytes 196616 | tf_op jit(solution)/shard_map/ppermute | solution.py:15
  36.8 10.6 %collective-permute-start.10 = (f32[8,66,1,128]{3,0,2,1:T(8,128)S(1)}, f32[8,66,1,128]{3,0,2,1:T(8,128)S(1)}, u32[]{:S(2)}, u32[]{:S(2)}) collective-permute-start(f32[8,66,1,128]{3,0,2,1:T(8,128)S(1)} %get-tuple-element.13), channel_id=1, source_target_pairs={{1,0},{2,1},{3,2},{4,3},{5,4},{6,5},{7,6},{9,8},{10,9},{11,10},{12... | collective-permute-start | bytes 811016 | tf_op jit(solution)/shard_map/ppermute | solution.py:18
  38.1 16.6 %collective-permute-start.11 = (f32[8,66,1,128]{3,0,2,1:T(8,128)S(1)}, f32[8,66,1,128]{3,0,2,1:T(8,128)S(1)}, u32[]{:S(2)}, u32[]{:S(2)}) collective-permute-start(f32[8,66,1,128]{3,0,2,1:T(8,128)S(1)} %get-tuple-element.14), channel_id=1, source_target_pairs={{0,1},{1,2},{2,3},{3,4},{4,5},{5,6},{6,7},{8,9},{9,10},{10,11},{11... | collective-permute-start | bytes 811016 | tf_op jit(solution)/shard_map/ppermute | solution.py:15
  62.1 30.0 %copy-start.2 = (f32[8,64,16,128]{3,0,2,1:T(8,128)}, f32[8,64,16,128]{3,0,2,1:T(8,128)S(1)}, u32[]{:S(2)}) copy-start(f32[8,64,16,128]{3,0,2,1:T(8,128)S(1)} %get-tuple-element.7) | copy-start | bytes 12582916
  62.1 30.0 %copy-start.4 = (f32[8,64,16,128]{3,0,2,1:T(8,128)}, f32[8,64,16,128]{3,0,2,1:T(8,128)S(1)}, u32[]{:S(2)}) copy-start(f32[8,64,16,128]{3,0,2,1:T(8,128)S(1)} %get-tuple-element.8) | copy-start | bytes 12582916
  62.1 4.3 %collective-permute-start.12 = (f32[8,1,16,128]{3,0,2,1:T(8,128)S(1)}, f32[8,1,16,128]{3,0,2,1:T(8,128)S(1)}, u32[]{:S(2)}, u32[]{:S(2)}) collective-permute-start(f32[8,1,16,128]{3,0,2,1:T(8,128)S(1)} %get-tuple-element.16), channel_id=1, source_target_pairs={{8,0},{16,8},{24,16},{9,1},{17,9},{25,17},{10,2},{18,10},{26,18},{... | collective-permute-start | bytes 196616 | tf_op jit(solution)/shard_map/ppermute | solution.py:18
  63.4 3.9 %collective-permute-start.13 = (f32[8,1,16,128]{3,0,2,1:T(8,128)S(1)}, f32[8,1,16,128]{3,0,2,1:T(8,128)S(1)}, u32[]{:S(2)}, u32[]{:S(2)}) collective-permute-start(f32[8,1,16,128]{3,0,2,1:T(8,128)S(1)} %get-tuple-element.15), channel_id=1, source_target_pairs={{0,8},{8,16},{16,24},{1,9},{9,17},{17,25},{2,10},{10,18},{18,26},{... | collective-permute-start | bytes 196616 | tf_op jit(solution)/shard_map/ppermute | solution.py:15
  67.4 17.5 %collective-permute-start.14 = (f32[8,66,1,128]{3,0,2,1:T(8,128)S(1)}, f32[8,66,1,128]{3,0,2,1:T(8,128)S(1)}, u32[]{:S(2)}, u32[]{:S(2)}) collective-permute-start(f32[8,66,1,128]{3,0,2,1:T(8,128)S(1)} %get-tuple-element.11), channel_id=1, source_target_pairs={{1,0},{2,1},{3,2},{4,3},{5,4},{6,5},{7,6},{9,8},{10,9},{11,10},{12... | collective-permute-start | bytes 811016 | tf_op jit(solution)/shard_map/ppermute | solution.py:18
  68.7 16.6 %collective-permute-start.15 = (f32[8,66,1,128]{3,0,2,1:T(8,128)S(1)}, f32[8,66,1,128]{3,0,2,1:T(8,128)S(1)}, u32[]{:S(2)}, u32[]{:S(2)}) collective-permute-start(f32[8,66,1,128]{3,0,2,1:T(8,128)S(1)} %get-tuple-element.12), channel_id=1, source_target_pairs={{0,1},{1,2},{2,3},{3,4},{4,5},{5,6},{6,7},{8,9},{9,10},{10,11},{11... | collective-permute-start | bytes 811016 | tf_op jit(solution)/shard_map/ppermute | solution.py:15
  92.1 2.0 %copy-start.5 = (f32[8,64,16,128]{3,0,2,1:T(8,128)}, f32[8,64,16,128]{3,0,2,1:T(8,128)S(1)}, u32[]{:S(2)}) copy-start(f32[8,64,16,128]{3,0,2,1:T(8,128)S(1)} %fusion.10) | copy-start | bytes 12582916
  158.5 7.5 %copy-start.1 = (f32[8,64,16,128]{3,0,2,1:T(8,128)S(1)}, f32[8,64,16,128]{3,0,2,1:T(8,128)}, u32[]{:S(2)}) copy-start(f32[8,64,16,128]{3,0,2,1:T(8,128)} %copy-done) | copy-start | bytes 12582916
  158.5 7.5 %copy-start.3 = (f32[8,64,16,128]{3,0,2,1:T(8,128)S(1)}, f32[8,64,16,128]{3,0,2,1:T(8,128)}, u32[]{:S(2)}) copy-start(f32[8,64,16,128]{3,0,2,1:T(8,128)} %copy-done.2) | copy-start | bytes 12582916
where the time goes:
time: 178 us; the launch traced here: 177 us
  starting transfers between devices  44.6 us (25%)
  blocking collectives  44.6 us (25%)
  matrix products  37.9 us (21%)
  other arithmetic  29 us (16%)
  waiting for transfers between devices  14.8 us (8%)
  local copies, waits for them, and re-layouts  5.36 us (3%)
    psum x1, blocking collectives, shards(): gram = lax.psum(gram_local, ('gx', 'gy'))  44.6 us
    ppermute x9, starting transfers between devices, padded_2(): lax.ppermute(lax.slice_in_dim(block, block.shape[dim] - width, None, axis...  35.5 us
    dot_general x1, matrix products, shards(): gram_local = jnp.einsum('aijk,bijk->ab', basis, basis, precision=highest)  11.2 us
    ppermute x9, waiting for transfers between devices, padded_2(): lax.ppermute(lax.slice_in_dim(block, block.shape[dim] - width, None, axis...  10.7 us
    dot_general x1, matrix products, shards(): project_local = jnp.einsum('aijk,bijk->ab', basis, image, precision=highest)  10.4 us
    ppermute x7, starting transfers between devices, padded_2(): lax.ppermute(lax.slice_in_dim(block, 0, width, axis=dim), axis, backward)  9.04 us
    dot_general x1, matrix products, shards(): jnp.einsum('ab,aijk->bijk', coeffs, basis, precision=highest)  8.56 us
    sub x1, other arithmetic, shards(): powered = applied - basis_shift * blocks  7.45 us
  transfers between devices with their start and end apart: 16, of which 6 were waited for; matrix products, arithmetic and copies ran while one was open for 7% of the time, Pallas kernels for 0%

commit v1 on v0

--- a/solution.py
+++ b/solution.py
@@ -77,7 +77,7 @@
     image = jnp.concatenate([applied, second], axis=0)
     gram_local = jnp.einsum("aijk,bijk->ab", basis, basis, precision=highest)
     project_local = jnp.einsum("aijk,bijk->ab", basis, image, precision=highest)
-    gram = lax.psum(gram_local, ("gx", "gy"))
+    gram = lax.psum(lax.psum(gram_local, "gx"), "gy")
     project = lax.psum(project_local, ("gx", "gy"))
     coeffs = finish(gram, project)
     new_iterates = iterates + jnp.einsum("ab,aijk->bijk", coeffs, basis, precision=highest)

time: 178 us -> 207 us (1.16)
  blocking collectives: 44.6 us -> 67.5 us
  other arithmetic: 29 us -> 32.1 us
  waiting for transfers between devices: 14.8 us -> 17.7 us
    psum x1 -> x3, blocking collectives: 44.6 us -> 67.5 us  [the longest x1 40.2 us: shards(): project = lax.psum(project_local, ('gx', 'gy'))]
    unnamed x26 -> x36, local copies, waits for them, and re-layouts: 4.88 us -> 4.92 us
  transfers between devices with their start and end apart: 16 -> 16, of which waited for: 6 -> 6; matrix products, arithmetic and copies ran while one was open for 7% -> 2% of each run, Pallas kernels for 0% -> 0%
where the time goes in v1:
time: 207 us; the launch traced here: 206 us
  blocking collectives  67.5 us (33%)
  starting transfers between devices  44.6 us (22%)
  matrix products  37.8 us (18%)
  other arithmetic  32.1 us (16%)
  waiting for transfers between devices  17.7 us (9%)
  local copies, waits for them, and re-layouts  5.41 us (3%)
    psum x1, blocking collectives, shards(): project = lax.psum(project_local, ('gx', 'gy'))  40.2 us
    ppermute x9, starting transfers between devices, padded_2(): lax.ppermute(lax.slice_in_dim(block, block.shape[dim] - width, None, axis...  35.1 us
    psum x2, blocking collectives, shards(): gram = lax.psum(lax.psum(gram_local, 'gx'), 'gy')  27.3 us
    ppermute x9, waiting for transfers between devices, padded_2(): lax.ppermute(lax.slice_in_dim(block, block.shape[dim] - width, None, axis...  11.7 us
    dot_general x1, matrix products, shards(): gram_local = jnp.einsum('aijk,bijk->ab', basis, basis, precision=highest)  11.2 us
    dot_general x1, matrix products, shards(): project_local = jnp.einsum('aijk,bijk->ab', basis, image, precision=highest)  10.4 us
    ppermute x7, starting transfers between devices, padded_2(): lax.ppermute(lax.slice_in_dim(block, 0, width, axis=dim), axis, backward)  9.5 us
    dot_general x1, matrix products, shards(): jnp.einsum('ab,aijk->bijk', coeffs, basis, precision=highest)  8.56 us
  transfers between devices with their start and end apart: 16, of which 6 were waited for; matrix products, arithmetic and copies ran while one was open for 2% of the time, Pallas kernels for 0%

profile of v1, /device:TPU:0, one launch (start us, length us, event | category | flops | bytes accessed | tf_op | source)
XLA Modules:
  0.0 206.2 jit_solution(17266462612329100155)
XLA Ops:
  0.7 2.7 %reduce_sum.18 = f32[64,16,128]{2,1,0:T(8,128)S(1)} reduce(f32[8,64,16,128]{3,2,1,0:T(8,128)} %param.13, f32[]{:T(128)} %constant.43.clone.1), dimensions={0}, to_apply=%region_0.0 | reduce | flops 917504 | bytes 4718596 | tf_op jit(solution)/shard_map/reduce_sum | solution.py:60
  4.7 3.0 %collective-permute-start.2 = (f32[1,16,128]{2,1,0:T(8,128)S(1)}, f32[1,16,128]{2,1,0:T(8,128)S(1)}, u32[]{:S(2)}, u32[]{:S(2)}) collective-permute-start(f32[1,16,128]{2,1,0:T(8,128)S(1)} %get-tuple-element.21), channel_id=1, source_target_pairs={{0,8},{8,16},{16,24},{1,9},{9,17},{17,25},{2,10},{10,18},{18,26},{... | collective-permute-start | bytes 24584 | tf_op jit(solution)/shard_map/ppermute | solution.py:15
  7.7 4.5 %collective-permute-start.4 = (f32[1,16,128]{2,1,0:T(8,128)S(1)}, f32[1,16,128]{2,1,0:T(8,128)S(1)}, u32[]{:S(2)}, u32[]{:S(2)}) collective-permute-start(f32[1,16,128]{2,1,0:T(8,128)S(1)} %get-tuple-element.20), channel_id=1, source_target_pairs={{0,8},{8,16},{16,24},{1,9},{9,17},{17,25},{2,10},{10,18},{18,26},{... | collective-permute-start | bytes 24584 | tf_op jit(solution)/shard_map/ppermute | solution.py:15
  13.6 3.0 %collective-permute-start.1 = (f32[1,16,128]{2,1,0:T(8,128)S(1)}, f32[1,16,128]{2,1,0:T(8,128)S(1)}, u32[]{:S(2)}, u32[]{:S(2)}) collective-permute-start(f32[1,16,128]{2,1,0:T(8,128)S(1)} %slice.156), channel_id=1, source_target_pairs={{0,8},{8,16},{16,24},{1,9},{9,17},{17,25},{2,10},{10,18},{18,26},{... | collective-permute-start | bytes 24584 | tf_op jit(solution)/shard_map/ppermute | solution.py:15
  18.1 4.5 %collective-permute-start.7 = (f32[66,1,128]{2,1,0:T(1,128)S(1)}, f32[66,1,128]{2,1,0:T(1,128)S(1)}, u32[]{:S(2)}, u32[]{:S(2)}) collective-permute-start(f32[66,1,128]{2,1,0:T(1,128)S(1)} %get-tuple-element.18), channel_id=1, source_target_pairs={{0,1},{1,2},{2,3},{3,4},{4,5},{5,6},{6,7},{8,9},{9,10},{10,11},{11... | collective-permute-start | bytes 101384 | tf_op jit(solution)/shard_map/ppermute | solution.py:15
  22.7 4.3 %collective-permute-start.6 = (f32[66,1,128]{2,1,0:T(1,128)S(1)}, f32[66,1,128]{2,1,0:T(1,128)S(1)}, u32[]{:S(2)}, u32[]{:S(2)}) collective-permute-start(f32[66,1,128]{2,1,0:T(1,128)S(1)} %slice.194), channel_id=1, source_target_pairs={{0,1},{1,2},{2,3},{3,4},{4,5},{5,6},{6,7},{8,9},{9,10},{10,11},{11... | collective-permute-start | bytes 101384 | tf_op jit(solution)/shard_map/ppermute | solution.py:15
  27.3 1.3 collective-permute-done.6
  28.6 1.6 fusion.33
  31.5 1.4 collective-permute-start.8
  33.0 3.0 %collective-permute-start.9 = (f32[8,1,16,128]{3,0,2,1:T(8,128)S(1)}, f32[8,1,16,128]{3,0,2,1:T(8,128)S(1)}, u32[]{:S(2)}, u32[]{:S(2)}) collective-permute-start(f32[8,1,16,128]{3,0,2,1:T(8,128)S(1)} %get-tuple-element.15), channel_id=1, source_target_pairs={{0,8},{8,16},{16,24},{1,9},{9,17},{17,25},{2,10},{10,18},{18,26},{... | collective-permute-start | bytes 196616 | tf_op jit(solution)/shard_map/ppermute | solution.py:15
  38.2 5.0 %collective-permute-start.11 = (f32[8,66,1,128]{3,0,2,1:T(8,128)S(1)}, f32[8,66,1,128]{3,0,2,1:T(8,128)S(1)}, u32[]{:S(2)}, u32[]{:S(2)}) collective-permute-start(f32[8,66,1,128]{3,0,2,1:T(8,128)S(1)} %get-tuple-element.12), channel_id=1, source_target_pairs={{0,1},{1,2},{2,3},{3,4},{4,5},{5,6},{6,7},{8,9},{9,10},{10,11},{11... | collective-permute-start | bytes 811016 | tf_op jit(solution)/shard_map/ppermute | solution.py:15
  43.5 4.0 %collective-permute-done.10 = f32[8,66,1,128]{3,0,2,1:T(8,128)S(1)} collective-permute-done((f32[8,66,1,128]{3,0,2,1:T(8,128)S(1)}, f32[8,66,1,128]{3,0,2,1:T(8,128)S(1)}, u32[]{:S(2)}, u32[]{:S(2)}) %collective-permute-start.10) | collective-permute-done | bytes 270368 | tf_op jit(solution)/shard_map/ppermute | solution.py:18
  47.6 7.2 %collective-permute-done.11 = f32[8,66,1,128]{3,0,2,1:T(8,128)S(1)} collective-permute-done((f32[8,66,1,128]{3,0,2,1:T(8,128)S(1)}, f32[8,66,1,128]{3,0,2,1:T(8,128)S(1)}, u32[]{:S(2)}, u32[]{:S(2)}) %collective-permute-start.11) | collective-permute-done | bytes 270368 | tf_op jit(solution)/shard_map/ppermute | solution.py:15
  54.8 8.3 %multiply_subtract_fusion = (f32[8,64,16,128]{3,0,2,1:T(8,128)S(1)}, f32[8,64,16,128]{3,0,2,1:T(8,128)}) fusion(f32[8,64,16]{0,2,1:T(8,128)S(1)} %fusion.43, f32[64,16,128]{2,1,0:T(8,128)S(1)} %get-tuple-element.7, f32[64,16,128]{2,1,0:T(8,128)S(1)} %pad.18, f32[8,64,16,128]{3,0,2,1:T(8,128)S(1)} %broadcast_multiply_fusion, f32[64,16,128]{2,1,0:T(8,128)S(1)} %copy-done.8, ...), kind=kLoop, calls=%fused_computation.51 | loop fusion | flops 25165824 | bytes 17481728 | tf_op jit(solution)/shard_map/sub | solution.py:73
  63.1 11.2 %fusion.28 = f32[16,16]{0,1:T(8,128)S(1)} fusion(f32[8,64,16,128]{3,0,2,1:T(8,128)S(1)} %get-tuple-element.5, f32[8,64,16,128]{3,0,2,1:T(8,128)S(1)} %broadcast_multiply_fusion), kind=kOutput, calls=%fused_computation.55 | convolution fusion | flops 404750336 | bytes 8389632 | tf_op jit(solution)/shard_map/aijk,bijk->ab/dot_general | solution.py:78
  74.3 1.3 collective-permute-start.12
  75.6 3.0 %collective-permute-start.13 = (f32[8,1,16,128]{3,0,2,1:T(8,128)S(1)}, f32[8,1,16,128]{3,0,2,1:T(8,128)S(1)}, u32[]{:S(2)}, u32[]{:S(2)}) collective-permute-start(f32[8,1,16,128]{3,0,2,1:T(8,128)S(1)} %get-tuple-element.13), channel_id=1, source_target_pairs={{0,8},{8,16},{16,24},{1,9},{9,17},{17,25},{2,10},{10,18},{18,26},{... | collective-permute-start | bytes 196616 | tf_op jit(solution)/shard_map/ppermute | solution.py:15
  78.6 7.3 %psum.21 = f32[16,16]{0,1:T(8,128)S(1)} all-reduce(f32[16,16]{0,1:T(8,128)S(1)} %fusion.28), channel_id=1, replica_groups=mesh['gx'=4,'gy'=8] {'gx'}, use_global_device_ids=true, to_apply=%region_1.2 | all-reduce | flops 256 | bytes 2048 | tf_op jit(solution)/shard_map/psum | solution.py:80
  85.9 20.0 %psum.22 = f32[16,16]{0,1:T(8,128)S(1)} all-reduce(f32[16,16]{0,1:T(8,128)S(1)} %psum.21), channel_id=1, replica_groups=mesh['gx'=4,'gy'=8] {'gy'}, use_global_device_ids=true, to_apply=%region_2.3 | all-reduce | flops 256 | bytes 2048 | tf_op jit(solution)/shard_map/psum | solution.py:80
  106.0 1.5 cholesky.44
  111.3 1.6 collective-permute-start.14
  112.9 4.6 %collective-permute-start.15 = (f32[8,66,1,128]{3,0,2,1:T(8,128)S(1)}, f32[8,66,1,128]{3,0,2,1:T(8,128)S(1)}, u32[]{:S(2)}, u32[]{:S(2)}) collective-permute-start(f32[8,66,1,128]{3,0,2,1:T(8,128)S(1)} %get-tuple-element.10), channel_id=1, source_target_pairs={{0,1},{1,2},{2,3},{3,4},{4,5},{5,6},{6,7},{8,9},{9,10},{10,11},{11... | collective-permute-start | bytes 811016 | tf_op jit(solution)/shard_map/ppermute | solution.py:15
  117.8 2.0 collective-permute-done.14
  119.8 2.2 %collective-permute-done.15 = f32[8,66,1,128]{3,0,2,1:T(8,128)S(1)} collective-permute-done((f32[8,66,1,128]{3,0,2,1:T(8,128)S(1)}, f32[8,66,1,128]{3,0,2,1:T(8,128)S(1)}, u32[]{:S(2)}, u32[]{:S(2)}) %collective-permute-start.15) | collective-permute-done | bytes 270368 | tf_op jit(solution)/shard_map/ppermute | solution.py:15
  122.0 7.9 %fusion.10 = f32[8,64,16,128]{3,0,2,1:T(8,128)S(1)} fusion(f32[8,64,16,128]{3,0,2,1:T(8,128)S(1)} %copy-done.4, f32[8,66,1,128]{3,0,2,1:T(8,128)S(1)} %collective-permute-done.15, f32[8,1,16,128]{3,0,2,1:T(8,128)S(1)} %collective-permute-done.12, f32[8,1,16,128]{3,0,2,1:T(8,128)S(1)} %collective-permute-done.13, ...), kind=kLoop, calls=%fused_computation.16 | loop fusion | flops 22020096 | bytes 12730368 | tf_op jit(solution)/shard_map/sub | solution.py:39
  129.9 2.0 copy-done.7
  131.8 10.4 %fusion.29 = f32[16,16]{1,0:T(8,128)S(1)} fusion(f32[8,64,16,128]{3,0,2,1:T(8,128)S(1)} %fusion.10, f32[8,64,16,128]{3,0,2,1:T(8,128)S(1)} %copy-done.6, f32[8,64,16,128]{3,0,2,1:T(8,128)S(1)} %copy-done.4, f32[8,64,16,128]{3,0,2,1:T(8,128)S(1)} %copy-done.1), kind=kOutput, calls=%fused_computation.56 | convolution fusion | flops 406847488 | bytes 16778240 | tf_op jit(solution)/shard_map/aijk,bijk->ab/dot_general | solution.py:79
  142.2 40.2 %psum.23 = f32[16,16]{1,0:T(8,128)S(1)} all-reduce(f32[16,16]{1,0:T(8,128)S(1)} %fusion.29), channel_id=1, replica_groups=mesh['gx'=4,'gy'=8] {'gx','gy'}, use_global_device_ids=true, to_apply=%region_5.7 | all-reduce | flops 256 | bytes 2048 | tf_op jit(solution)/shard_map/psum | solution.py:81
  182.8 1.5 cholesky.55
  187.4 6.6 %fusion = f32[1,64,16,128]{3,0,2,1:T(1,128)S(1)} fusion(f32[8,64,16,128]{3,0,2,1:T(8,128)} %copy-done.7, f32[8,64,16,128]{3,0,2,1:T(8,128)} %get-tuple-element.6, f32[16]{0:T(128)S(1)} %get-tuple-element.23), kind=kOutput, calls=%fused_computation.6 | convolution fusion | flops 27262976 | bytes 8912960 | tf_op jit(solution)/shard_map/a,aijk->ijk/dot_general | solution.py:85
  194.9 8.6 %copy_add_fusion = f32[8,64,16,128]{3,0,2,1:T(8,128)S(1)} fusion(f32[8,64,16,128]{3,2,1,0:T(8,128)} %param.13, f32[8,64,16,128]{3,0,2,1:T(8,128)S(1)} %copy-done.5, f32[8,64,16,128]{3,0,2,1:T(8,128)S(1)} %copy-done.2, f32[16,8]{0,1:T(8,128)S(1)} %get-tuple-element.24), kind=kOutput, calls=%fused_computation.50 | convolution fusion | flops 204472320 | bytes 16777728 | tf_op jit(solution)/shard_map/ab,aijk->bijk/dot_general | solution.py:83
  203.4 2.8 %copy.15 = f32[8,64,16,128]{3,2,1,0:T(8,128)} copy(f32[8,64,16,128]{3,0,2,1:T(8,128)S(1)} %copy_add_fusion) | data formatting | bytes 8388608
  (85 shorter events, 16.7 us)
Async XLA Ops:
  0.6 7.1 %copy-start.9 = (f32[64,16,128]{2,1,0:T(8,128)S(1)}, f32[64,16,128]{2,1,0:T(8,128)}, u32[]{:S(2)}) copy-start(f32[64,16,128]{2,1,0:T(8,128)} %param.11) | copy-start | bytes 1572868
  0.6 12.9 %copy-start.10 = (f32[64,16,128]{2,1,0:T(8,128)S(1)}, f32[64,16,128]{2,1,0:T(8,128)}, u32[]{:S(2)}) copy-start(f32[64,16,128]{2,1,0:T(8,128)} %param.10) | copy-start | bytes 1572868
  0.7 16.0 %copy-start.15 = (s32[64,16]{0,1:T(8,128)S(1)}, s32[64,16]{0,1:T(8,128)}, u32[]{:S(2)}) copy-start(s32[64,16]{0,1:T(8,128)} %param.14) | copy-start | bytes 12292
  0.7 28.0 %copy-start.8 = (f32[64,16,128]{2,1,0:T(8,128)S(1)}, f32[64,16,128]{2,1,0:T(8,128)}, u32[]{:S(2)}) copy-start(f32[64,16,128]{2,1,0:T(8,128)} %param.12) | copy-start | bytes 1572868
  0.7 28.0 %copy-start.11 = (f32[64,16,128]{2,1,0:T(8,128)S(1)}, f32[64,16,128]{2,1,0:T(8,128)}, u32[]{:S(2)}) copy-start(f32[64,16,128]{2,1,0:T(8,128)} %param.9) | copy-start | bytes 1572868
  3.4 13.3 %collective-permute-start = (f32[1,16,128]{2,1,0:T(8,128)S(1)}, f32[1,16,128]{2,1,0:T(8,128)S(1)}, u32[]{:S(2)}, u32[]{:S(2)}) collective-permute-start(f32[1,16,128]{2,1,0:T(8,128)S(1)} %get-tuple-element.22), channel_id=1, source_target_pairs={{8,0},{16,8},{24,16},{9,1},{17,9},{25,17},{10,2},{18,10},{26,18},{... | collective-permute-start | bytes 24584 | tf_op jit(solution)/shard_map/ppermute | solution.py:18
  4.7 12.0 %collective-permute-start.2 = (f32[1,16,128]{2,1,0:T(8,128)S(1)}, f32[1,16,128]{2,1,0:T(8,128)S(1)}, u32[]{:S(2)}, u32[]{:S(2)}) collective-permute-start(f32[1,16,128]{2,1,0:T(8,128)S(1)} %get-tuple-element.21), channel_id=1, source_target_pairs={{0,8},{8,16},{16,24},{1,9},{9,17},{17,25},{2,10},{10,18},{18,26},{... | collective-permute-start | bytes 24584 | tf_op jit(solution)/shard_map/ppermute | solution.py:15
  7.7 14.9 %collective-permute-start.4 = (f32[1,16,128]{2,1,0:T(8,128)S(1)}, f32[1,16,128]{2,1,0:T(8,128)S(1)}, u32[]{:S(2)}, u32[]{:S(2)}) collective-permute-start(f32[1,16,128]{2,1,0:T(8,128)S(1)} %get-tuple-element.20), channel_id=1, source_target_pairs={{0,8},{8,16},{16,24},{1,9},{9,17},{17,25},{2,10},{10,18},{18,26},{... | collective-permute-start | bytes 24584 | tf_op jit(solution)/shard_map/ppermute | solution.py:15
  12.2 10.4 %collective-permute-start.5 = (f32[1,16,128]{2,1,0:T(8,128)S(1)}, f32[1,16,128]{2,1,0:T(8,128)S(1)}, u32[]{:S(2)}, u32[]{:S(2)}) collective-permute-start(f32[1,16,128]{2,1,0:T(8,128)S(1)} %get-tuple-element.19), channel_id=1, source_target_pairs={{8,0},{16,8},{24,16},{9,1},{17,9},{25,17},{10,2},{18,10},{26,18},{... | collective-permute-start | bytes 24584 | tf_op jit(solution)/shard_map/ppermute | solution.py:18
  13.6 13.7 %collective-permute-start.1 = (f32[1,16,128]{2,1,0:T(8,128)S(1)}, f32[1,16,128]{2,1,0:T(8,128)S(1)}, u32[]{:S(2)}, u32[]{:S(2)}) collective-permute-start(f32[1,16,128]{2,1,0:T(8,128)S(1)} %slice.156), channel_id=1, source_target_pairs={{0,8},{8,16},{16,24},{1,9},{9,17},{17,25},{2,10},{10,18},{18,26},{... | collective-permute-start | bytes 24584 | tf_op jit(solution)/shard_map/ppermute | solution.py:15
  16.8 10.5 %collective-permute-start.3 = (f32[66,1,128]{2,1,0:T(1,128)S(1)}, f32[66,1,128]{2,1,0:T(1,128)S(1)}, u32[]{:S(2)}, u32[]{:S(2)}) collective-permute-start(f32[66,1,128]{2,1,0:T(1,128)S(1)} %get-tuple-element.17), channel_id=1, source_target_pairs={{1,0},{2,1},{3,2},{4,3},{5,4},{6,5},{7,6},{9,8},{10,9},{11,10},{12... | collective-permute-start | bytes 101384 | tf_op jit(solution)/shard_map/ppermute | solution.py:18
  18.1 9.2 %collective-permute-start.7 = (f32[66,1,128]{2,1,0:T(1,128)S(1)}, f32[66,1,128]{2,1,0:T(1,128)S(1)}, u32[]{:S(2)}, u32[]{:S(2)}) collective-permute-start(f32[66,1,128]{2,1,0:T(1,128)S(1)} %get-tuple-element.18), channel_id=1, source_target_pairs={{0,1},{1,2},{2,3},{3,4},{4,5},{5,6},{6,7},{8,9},{9,10},{10,11},{11... | collective-permute-start | bytes 101384 | tf_op jit(solution)/shard_map/ppermute | solution.py:15
  22.7 5.9 %collective-permute-start.6 = (f32[66,1,128]{2,1,0:T(1,128)S(1)}, f32[66,1,128]{2,1,0:T(1,128)S(1)}, u32[]{:S(2)}, u32[]{:S(2)}) collective-permute-start(f32[66,1,128]{2,1,0:T(1,128)S(1)} %slice.194), channel_id=1, source_target_pairs={{0,1},{1,2},{2,3},{3,4},{4,5},{5,6},{6,7},{8,9},{9,10},{10,11},{11... | collective-permute-start | bytes 101384 | tf_op jit(solution)/shard_map/ppermute | solution.py:15
  30.2 24.6 %copy-start.14 = (f32[64,16,128]{2,1,0:T(8,128)}, f32[64,16,128]{2,1,0:T(8,128)S(1)}, u32[]{:S(2)}) copy-start(f32[64,16,128]{2,1,0:T(8,128)S(1)} %get-tuple-element.8) | copy-start | bytes 1572868
  31.5 31.6 %copy-start = (f32[8,64,16,128]{3,0,2,1:T(8,128)}, f32[8,64,16,128]{3,0,2,1:T(8,128)S(1)}, u32[]{:S(2)}) copy-start(f32[8,64,16,128]{3,0,2,1:T(8,128)S(1)} %broadcast_multiply_fusion) | copy-start | bytes 12582916
  31.5 23.3 %copy-start.12 = (f32[64,16,128]{2,1,0:T(8,128)S(1)}, f32[64,16,128]{2,1,0:T(8,128)}, u32[]{:S(2)}) copy-start(f32[64,16,128]{2,1,0:T(8,128)} %param.9) | copy-start | bytes 1572868
  31.5 4.5 %collective-permute-start.8 = (f32[8,1,16,128]{3,0,2,1:T(8,128)S(1)}, f32[8,1,16,128]{3,0,2,1:T(8,128)S(1)}, u32[]{:S(2)}, u32[]{:S(2)}) collective-permute-start(f32[8,1,16,128]{3,0,2,1:T(8,128)S(1)} %get-tuple-element.16), channel_id=1, source_target_pairs={{8,0},{16,8},{24,16},{9,1},{17,9},{25,17},{10,2},{18,10},{26,18},{... | collective-permute-start | bytes 196616 | tf_op jit(solution)/shard_map/ppermute | solution.py:18
  33.0 3.9 %collective-permute-start.9 = (f32[8,1,16,128]{3,0,2,1:T(8,128)S(1)}, f32[8,1,16,128]{3,0,2,1:T(8,128)S(1)}, u32[]{:S(2)}, u32[]{:S(2)}) collective-permute-start(f32[8,1,16,128]{3,0,2,1:T(8,128)S(1)} %get-tuple-element.15), channel_id=1, source_target_pairs={{0,8},{8,16},{16,24},{1,9},{9,17},{17,25},{2,10},{10,18},{18,26},{... | collective-permute-start | bytes 196616 | tf_op jit(solution)/shard_map/ppermute | solution.py:15
  36.9 10.6 %collective-permute-start.10 = (f32[8,66,1,128]{3,0,2,1:T(8,128)S(1)}, f32[8,66,1,128]{3,0,2,1:T(8,128)S(1)}, u32[]{:S(2)}, u32[]{:S(2)}) collective-permute-start(f32[8,66,1,128]{3,0,2,1:T(8,128)S(1)} %get-tuple-element.11), channel_id=1, source_target_pairs={{1,0},{2,1},{3,2},{4,3},{5,4},{6,5},{7,6},{9,8},{10,9},{11,10},{12... | collective-permute-start | bytes 811016 | tf_op jit(solution)/shard_map/ppermute | solution.py:18
  38.2 16.6 %collective-permute-start.11 = (f32[8,66,1,128]{3,0,2,1:T(8,128)S(1)}, f32[8,66,1,128]{3,0,2,1:T(8,128)S(1)}, u32[]{:S(2)}, u32[]{:S(2)}) collective-permute-start(f32[8,66,1,128]{3,0,2,1:T(8,128)S(1)} %get-tuple-element.12), channel_id=1, source_target_pairs={{0,1},{1,2},{2,3},{3,4},{4,5},{5,6},{6,7},{8,9},{9,10},{10,11},{11... | collective-permute-start | bytes 811016 | tf_op jit(solution)/shard_map/ppermute | solution.py:15
  63.1 11.2 %copy-start.3 = (f32[8,64,16,128]{3,0,2,1:T(8,128)}, f32[8,64,16,128]{3,0,2,1:T(8,128)S(1)}, u32[]{:S(2)}) copy-start(f32[8,64,16,128]{3,0,2,1:T(8,128)S(1)} %get-tuple-element.5) | copy-start | bytes 12582916
  74.3 35.8 %collective-permute-start.12 = (f32[8,1,16,128]{3,0,2,1:T(8,128)S(1)}, f32[8,1,16,128]{3,0,2,1:T(8,128)S(1)}, u32[]{:S(2)}, u32[]{:S(2)}) collective-permute-start(f32[8,1,16,128]{3,0,2,1:T(8,128)S(1)} %get-tuple-element.14), channel_id=1, source_target_pairs={{8,0},{16,8},{24,16},{9,1},{17,9},{25,17},{10,2},{18,10},{26,18},{... | collective-permute-start | bytes 196616 | tf_op jit(solution)/shard_map/ppermute | solution.py:18
  75.6 34.5 %collective-permute-start.13 = (f32[8,1,16,128]{3,0,2,1:T(8,128)S(1)}, f32[8,1,16,128]{3,0,2,1:T(8,128)S(1)}, u32[]{:S(2)}, u32[]{:S(2)}) collective-permute-start(f32[8,1,16,128]{3,0,2,1:T(8,128)S(1)} %get-tuple-element.13), channel_id=1, source_target_pairs={{0,8},{8,16},{16,24},{1,9},{9,17},{17,25},{2,10},{10,18},{18,26},{... | collective-permute-start | bytes 196616 | tf_op jit(solution)/shard_map/ppermute | solution.py:15
  110.0 11.9 %copy-start.4 = (f32[8,64,16,128]{3,0,2,1:T(8,128)S(1)}, f32[8,64,16,128]{3,0,2,1:T(8,128)}, u32[]{:S(2)}) copy-start(f32[8,64,16,128]{3,0,2,1:T(8,128)} %copy-done.3) | copy-start | bytes 12582916
  110.1 11.9 %copy-start.13 = (f32[64,16,128]{2,1,0:T(8,128)S(1)}, f32[64,16,128]{2,1,0:T(8,128)}, u32[]{:S(2)}) copy-start(f32[64,16,128]{2,1,0:T(8,128)} %param.9) | copy-start | bytes 1572868
  111.3 8.5 %collective-permute-start.14 = (f32[8,66,1,128]{3,0,2,1:T(8,128)S(1)}, f32[8,66,1,128]{3,0,2,1:T(8,128)S(1)}, u32[]{:S(2)}, u32[]{:S(2)}) collective-permute-start(f32[8,66,1,128]{3,0,2,1:T(8,128)S(1)} %get-tuple-element.9), channel_id=1, source_target_pairs={{1,0},{2,1},{3,2},{4,3},{5,4},{6,5},{7,6},{9,8},{10,9},{11,10},{12... | collective-permute-start | bytes 811016 | tf_op jit(solution)/shard_map/ppermute | solution.py:18
  112.9 9.1 %collective-permute-start.15 = (f32[8,66,1,128]{3,0,2,1:T(8,128)S(1)}, f32[8,66,1,128]{3,0,2,1:T(8,128)S(1)}, u32[]{:S(2)}, u32[]{:S(2)}) collective-permute-start(f32[8,66,1,128]{3,0,2,1:T(8,128)S(1)} %get-tuple-element.10), channel_id=1, source_target_pairs={{0,1},{1,2},{2,3},{3,4},{4,5},{5,6},{6,7},{8,9},{9,10},{10,11},{11... | collective-permute-start | bytes 811016 | tf_op jit(solution)/shard_map/ppermute | solution.py:15
  117.8 14.0 %copy-start.1 = (f32[8,64,16,128]{3,0,2,1:T(8,128)S(1)}, f32[8,64,16,128]{3,0,2,1:T(8,128)}, u32[]{:S(2)}) copy-start(f32[8,64,16,128]{3,0,2,1:T(8,128)} %copy-done) | copy-start | bytes 12582916
  117.8 14.0 %copy-start.6 = (f32[8,64,16,128]{3,0,2,1:T(8,128)S(1)}, f32[8,64,16,128]{3,0,2,1:T(8,128)}, u32[]{:S(2)}) copy-start(f32[8,64,16,128]{3,0,2,1:T(8,128)} %get-tuple-element.6) | copy-start | bytes 12582916
  129.9 2.0 copy-start.7
  187.4 7.5 %copy-start.2 = (f32[8,64,16,128]{3,0,2,1:T(8,128)S(1)}, f32[8,64,16,128]{3,0,2,1:T(8,128)}, u32[]{:S(2)}) copy-start(f32[8,64,16,128]{3,0,2,1:T(8,128)} %copy-done) | copy-start | bytes 12582916
  187.4 7.5 %copy-start.5 = (f32[8,64,16,128]{3,0,2,1:T(8,128)S(1)}, f32[8,64,16,128]{3,0,2,1:T(8,128)}, u32[]{:S(2)}) copy-start(f32[8,64,16,128]{3,0,2,1:T(8,128)} %copy-done.3) | copy-start | bytes 12582916
